TPU v7x, 256 devices: a whole 4x4x8 slice. The times are simulated.
256 devices in a mesh: gx: 4 (over y_lo, core), gy: 8 (over z), gz: 8 (over y_hi, x).
Axes of the slice: x: 4, y: 4 (y_hi: 2, y_lo: 2; y = y_hi * 2 + y_lo), z: 8, core: 2. Of those that a mesh axis runs over, the one named last changes fastest.
Arguments:
- block: float32 [32, 64, 64, 256], P('gx', 'gy', 'gz'), may hold values from -8 to 8
- onsite: float32 [32, 64, 64], P('gx', 'gy', 'gz'), may hold values from -8 to 8
- hopping: float32 [13], replicated, may hold values from -1 to 1
- cut_frac: float32 [1], replicated, may hold values from -0.5 to 0
Outputs:
- states: float32 [32, 64, 64, 256], P('gx', 'gy', 'gz')
- projected: float32 [256, 256], replicated
- factor: float32 [256, 256], replicated
All inputs are finite; a program needn't handle non-finite values. Where the computation divides by a largest or mean magnitude, that divisor is 1e-20 or more.
Results may differ from a plain program's by a relative error of at most 0.0008.
Values sent between devices are 32-bit elements; how exact they have to be, the bound alone decides.
A program may use at most 64 MiB of HBM per device.

v0:
```python
import jax
import jax.numpy as jnp
from jax import lax
from jax.sharding import PartitionSpec as P

DEG = 4


def extended(block, sides, width):
    for axis, dim in sides:
        count = lax.axis_size(axis)
        forward = [(i, i + 1) for i in range(count - 1)]
        backward = [(target, source) for source, target in forward]
        low = lax.ppermute(
            lax.slice_in_dim(block, block.shape[dim] - width, None, axis=dim), axis, forward
        )
        high = lax.ppermute(lax.slice_in_dim(block, 0, width, axis=dim), axis, backward)
        block = jnp.concatenate([low, block, high], axis=dim)
    return block


def half_offsets():
    result = []
    for dx in (-1, 0, 1):
        for dy in (-1, 0, 1):
            for dz in (-1, 0, 1):
                if (dx, dy, dz) > (0, 0, 0):
                    result.append((dx, dy, dz))
    return result


def stencil(padded, field, onsite, hopping):
    size_x, size_y, size_z = (field.shape[0], field.shape[1], field.shape[2])
    total = onsite[:, :, :, None] * field
    for index, offset in enumerate(half_offsets()):
        for sign in (1, -1):
            ax_x, ax_y, ax_z = (1 + sign * offset[0], 1 + sign * offset[1], 1 + sign * offset[2])
            total = (
                total
                + hopping[index]
                * padded[ax_x : ax_x + size_x, ax_y : ax_y + size_y, ax_z : ax_z + size_z]
            )
    return total


def apply_ham(field, onsite, hopping):
    padded = extended(field, (("gx", 0), ("gy", 1), ("gz", 2)), 1)
    return stencil(padded, field, onsite, hopping)


def cheb_filter(field, operate, bound, cut):
    half_width = (bound - cut) / 2.0
    center = (bound + cut) / 2.0
    sigma = half_width / (-bound - center)
    sigma_one = sigma
    older = field
    newer = sigma / half_width * (operate(older) - center * older)
    for step in range(DEG - 1):
        sigma_next = 1.0 / (2.0 / sigma_one - sigma)
        nextone = (
            2.0 * sigma_next / half_width * (operate(newer) - center * newer)
            - sigma * sigma_next * older
        )
        older, newer, sigma = (newer, nextone, sigma_next)
    return newer


def gram_of(left, right):
    return lax.dot_general(
        left,
        right,
        (((0,), (0,)), ((), ())),
        precision=lax.Precision.HIGHEST,
        preferred_element_type=jnp.float32,
    )


def lower_and_inverse(gram):
    lower = jnp.linalg.cholesky(gram)
    ident = jnp.eye(gram.shape[0], dtype=jnp.float32)
    return (lower, jax.scipy.linalg.solve_triangular(lower, ident, lower=True))


def rotate(flat, factor):
    return jnp.dot(
        flat, factor.T, precision=lax.Precision.HIGHEST, preferred_element_type=jnp.float32
    )


def body(block, onsite, hopping, cut_frac):
    shape = block.shape
    size_x, size_y, size_z, columns = shape
    total_sites = (
        size_x * size_y * size_z * lax.axis_size("gx") * lax.axis_size("gy") * lax.axis_size("gz")
    )
    largest = lax.pmax(jnp.max(jnp.abs(onsite)), ("gx", "gy", "gz"))
    bound = largest + 2.0 * jnp.sum(jnp.abs(hopping))
    cut = cut_frac[0] * bound
    filtered = cheb_filter(block, lambda field: apply_ham(field, onsite, hopping), bound, cut)
    flat = filtered.reshape(-1, columns)
    gram_one = lax.psum(gram_of(flat, flat), ("gx", "gy", "gz")) / total_sites
    lower_one, inverse_one = lower_and_inverse(gram_one)
    first = rotate(flat, inverse_one)
    gram_two = lax.psum(gram_of(first, first), ("gx", "gy", "gz")) / total_sites
    lower_two, factor_two = lower_and_inverse(gram_two)
    states = rotate(first, factor_two)
    image = apply_ham(states.reshape(shape), onsite, hopping).reshape(-1, columns)
    projected = lax.psum(gram_of(states, image), ("gx", "gy", "gz")) / total_sites
    return (states.reshape(shape), projected, lower_one)


def solution(mesh):
    return jax.shard_map(
        body,
        mesh=mesh,
        in_specs=(P("gx", "gy", "gz", None), P("gx", "gy", "gz"), P(), P()),
        out_specs=(P("gx", "gy", "gz", None), P(), P()),
        check_vma=False,
    )
```

profile of v0, /device:TPU:2, one launch (start us, length us, event | category | flops | bytes accessed | tf_op | source)
XLA Modules:
  0.0 1180.9 jit_solution(2709486755815399544)
XLA Ops:
  12.5 80.9 %pmax.7 = f32[]{:T(128)} all-reduce(f32[]{:T(128)} %abs_reduce_fusion), channel_id=1, replica_groups=mesh['gx'=4,'gy'=8,'gz'=8] {'gx','gy','gz'}, use_global_device_ids=true, to_apply=%region_1.0 | all-reduce | flops 1 | bytes 8 | tf_op jit(solution)/shard_map/pmax | solution.py:96
  96.6 4.6 collective-permute-start.2
  113.9 10.0 fusion.160
  130.4 4.9 collective-permute-start.8
  146.7 10.0 fusion.124
  163.3 5.0 collective-permute-start.14
  180.1 10.0 fusion.93
  196.7 5.1 collective-permute-start.20
  205.9 7.8 collective-permute-start.23
  216.5 10.0 fusion.62
  228.8 269.9 %all-reduce.5.cloned.1.call-done = f32[256,256]{0,1:T(8,128)} async-done(((f32[256,256]{0,1:T(8,128)}), f32[256,256]{0,1:T(8,128)}) %all-reduce.5.cloned.1.call-update) | async-done | bytes 262160 | tf_op jit(solution)/shard_map/psum | solution.py:101
  500.8 11.7 cholesky.130
  512.6 9.8 custom-call.13
  522.9 11.7 cholesky.147
  541.4 19.7 %custom-call.14 = f32[2,128,128]{1,2,0:T(8,128)S(1)} custom-call(f32[2,128,128]{2,1,0:T(8,128)S(1)} %get-tuple-element.19), custom_call_target="InvertDiagBlocksLowerTriangular" | custom-call | tf_op jit(solution)/shard_map/jit(_solve_triangular)/triangular_solve | solution.py:81
  564.4 249.0 %all-reduce.7.cloned.1.call-done = f32[256,256]{0,1:T(8,128)} async-done(((f32[256,256]{0,1:T(8,128)}), f32[256,256]{0,1:T(8,128)}) %all-reduce.7.cloned.1.call-update) | async-done | bytes 262160 | tf_op jit(solution)/shard_map/psum | solution.py:104
  815.6 11.7 cholesky.164
  827.3 9.8 custom-call.15
  837.6 11.7 cholesky.181
  851.9 4.1 while.5
  856.0 19.7 %custom-call.16 = f32[2,128,128]{1,2,0:T(8,128)S(1)} custom-call(f32[2,128,128]{2,1,0:T(8,128)S(1)} %get-tuple-element.20), custom_call_target="InvertDiagBlocksLowerTriangular" | custom-call | tf_op jit(solution)/shard_map/jit(_solve_triangular)/triangular_solve | solution.py:81
  883.8 4.6 collective-permute-start.26
  900.6 10.0 fusion.31
  912.3 260.0 %all-reduce.9.cloned.1.call-done = f32[256,256]{0,1:T(8,128)} async-done(((f32[256,256]{0,1:T(8,128)}), f32[256,256]{0,1:T(8,128)}) %all-reduce.9.cloned.1.call-update) | async-done | bytes 262160 | tf_op jit(solution)/shard_map/psum | solution.py:108
  (152 shorter events, 117.0 us)
Async XLA Ops:
  7.2 491.5 %all-reduce.5.cloned.1.call-start = ((), (), s32[]{:S(2)}) async-start(), calls=%async_computation | async-start | bytes 524288 | tf_op jit(solution)/shard_map/psum | solution.py:101
  8.1 86.0 %collective-permute-start = (f32[1,8,8,256]{3,2,1,0:T(8,128)S(1)}, f32[1,8,8,256]{3,2,1,0:T(8,128)S(1)}, u32[]{:S(2)}, u32[]{:S(2)}) collective-permute-start(f32[1,8,8,256]{3,2,1,0:T(8,128)S(1)} %get-tuple-element.93), channel_id=1, source_target_pairs={{0,64},{64,128},{128,192},{1,65},{65,129},{129,193},{2,66},{66,130... | collective-permute-start | bytes 196616 | tf_op jit(solution)/shard_map/ppermute | solution.py:14
  11.2 84.0 %collective-permute-start.1 = (f32[1,8,8,256]{3,2,1,0:T(8,128)S(1)}, f32[1,8,8,256]{3,2,1,0:T(8,128)S(1)}, u32[]{:S(2)}, u32[]{:S(2)}) collective-permute-start(f32[1,8,8,256]{3,2,1,0:T(8,128)S(1)} %get-tuple-element.92), channel_id=1, source_target_pairs={{64,0},{128,64},{192,128},{65,1},{129,65},{193,129},{66,2},{130,66... | collective-permute-start | bytes 196616 | tf_op jit(solution)/shard_map/ppermute | solution.py:17
  95.3 7.8 collective-permute-start.3
  96.6 6.6 collective-permute-start.2
  103.3 6.6 collective-permute-start.4
  129.1 7.3 collective-permute-start.9
  130.4 7.2 collective-permute-start.8
  137.8 6.6 collective-permute-start.10
  139.7 6.6 collective-permute-start.11
  162.0 6.8 collective-permute-start.15
  163.3 7.1 collective-permute-start.14
  170.5 6.8 collective-permute-start.16
  172.5 7.2 collective-permute-start.17
  195.4 6.9 collective-permute-start.21
  196.7 7.2 collective-permute-start.20
  204.0 10.5 collective-permute-start.22
  205.9 10.1 collective-permute-start.23
  228.2 585.2 %all-reduce.7.cloned.1.call-start = ((), (), s32[]{:S(2)}) async-start(), calls=%async_computation.1 | async-start | bytes 524288 | tf_op jit(solution)/shard_map/psum | solution.py:104
  564.4 607.9 %all-reduce.9.cloned.1.call-start = ((), (), s32[]{:S(2)}) async-start(), calls=%async_computation.2 | async-start | bytes 524288 | tf_op jit(solution)/shard_map/psum | solution.py:108
  882.5 7.1 collective-permute-start.27
  883.8 7.2 collective-permute-start.26
  891.1 6.6 collective-permute-start.28
  893.3 6.8 collective-permute-start.29
  (13 other events, 175.0 us)
Sparse Core Ops, SparseCore 0:
  228.4 270.3 all-reduce.4
  564.5 248.9 all-reduce.6
  912.5 259.8 all-reduce.8
where the time goes:
time: 1190 us; the launch traced here: 1180 us
  waiting for transfers between devices  806 us (68%)
  other arithmetic  169 us (14%)
  starting transfers between devices  84.7 us (7%)
  blocking collectives  80.9 us (7%)
  between operations  19.6 us (2%)
    psum x1, waiting for transfers between devices, body(): gram_one = lax.psum(gram_of(flat, flat), ('gx', 'gy', 'gz')) / total_sites  270 us
    psum x1, waiting for transfers between devices, body(): lax.psum(gram_of(states, image), ('gx', 'gy', 'gz')) / total_sites  260 us
    psum x1, waiting for transfers between devices, body(): gram_two = lax.psum(gram_of(first, first), ('gx', 'gy', 'gz')) / total_sites  249 us
    pmax x1, blocking collectives, body(): largest = lax.pmax(jnp.max(jnp.abs(onsite)), ('gx', 'gy', 'gz'))  80.9 us
    another operation x13, other arithmetic, lower_and_inverse(): lower = jnp.linalg.cholesky(gram)  68.5 us
    ppermute x15, starting transfers between devices, extended(): lax.ppermute(lax.slice_in_dim(block, block.shape[dim] - width, None, axis...  59.6 us
    another operation x5, other arithmetic, lower_and_inverse(): return (lower, jax.scipy.linalg.solve_triangular(lower, ident, lower=True))  40.1 us
    sub x3, other arithmetic, cheb_filter(): 2.0 * sigma_next / half_width * (operate(newer) - center * newer)  30.1 us
  transfers between devices with their start and end apart: 33, of which 25 were waited for; matrix products, arithmetic and copies ran while one was open for 0% of the time, Pallas kernels for 0%

commit v1 on v0

--- a/solution.py
+++ b/solution.py
@@ -98,7 +98,7 @@
     cut = cut_frac[0] * bound
     filtered = cheb_filter(block, lambda field: apply_ham(field, onsite, hopping), bound, cut)
     flat = filtered.reshape(-1, columns)
-    gram_one = lax.psum(gram_of(flat, flat), ("gx", "gy", "gz")) / total_sites
+    gram_one = lax.psum(lax.psum(gram_of(flat, flat), ("gy", "gz")), "gx") / total_sites
     lower_one, inverse_one = lower_and_inverse(gram_one)
     first = rotate(flat, inverse_one)
     gram_two = lax.psum(gram_of(first, first), ("gx", "gy", "gz")) / total_sites

time: 1190 us -> 1630 us (1.37)
  waiting for transfers between devices: 806 us -> 1240 us
    psum x1 -> x2, waiting for transfers between devices: 270 us -> 704 us  [the longest x1 658 us: body(): lax.psum(gram_of(flat, flat), ('gy', 'gz'))]
  transfers between devices with their start and end apart: 33 -> 34, of which waited for: 25 -> 26; matrix products, arithmetic and copies ran while one was open for 0% -> 0% of each run, Pallas kernels for 0% -> 0%
where the time goes in v1:
time: 1630 us; the launch traced here: 1620 us
  waiting for transfers between devices  1240 us (76%)
  other arithmetic  169 us (10%)
  starting transfers between devices  84.7 us (5%)
  blocking collectives  80.9 us (5%)
  between operations  19.6 us (1%)
    psum x1, waiting for transfers between devices, body(): lax.psum(gram_of(flat, flat), ('gy', 'gz'))  658 us
    psum x1, waiting for transfers between devices, body(): lax.psum(gram_of(states, image), ('gx', 'gy', 'gz')) / total_sites  260 us
    psum x1, waiting for transfers between devices, body(): gram_two = lax.psum(gram_of(first, first), ('gx', 'gy', 'gz')) / total_sites  251 us
    pmax x1, blocking collectives, body(): largest = lax.pmax(jnp.max(jnp.abs(onsite)), ('gx', 'gy', 'gz'))  80.9 us
    another operation x13, other arithmetic, lower_and_inverse(): lower = jnp.linalg.cholesky(gram)  68.5 us
    ppermute x15, starting transfers between devices, extended(): lax.ppermute(lax.slice_in_dim(block, block.shape[dim] - width, None, axis...  59.6 us
    psum x1, waiting for transfers between devices, body(): lax.psum(lax.psum(gram_of(flat, flat), ('gy', 'gz')), 'gx') / total_sites  45.1 us
    another operation x5, other arithmetic, lower_and_inverse(): return (lower, jax.scipy.linalg.solve_triangular(lower, ident, lower=True))  40.1 us
  transfers between devices with their start and end apart: 34, of which 26 were waited for; matrix products, arithmetic and copies ran while one was open for 0% of the time, Pallas kernels for 0%

profile of v1, /device:TPU:2, one launch (start us, length us, event | category | flops | bytes accessed | tf_op | source)
XLA Modules:
  0.0 1616.5 jit_solution(6528486332532541771)
XLA Ops:
  12.5 80.9 %pmax.7 = f32[]{:T(128)} all-reduce(f32[]{:T(128)} %abs_reduce_fusion), channel_id=1, replica_groups=mesh['gx'=4,'gy'=8,'gz'=8] {'gx','gy','gz'}, use_global_device_ids=true, to_apply=%region_1.0 | all-reduce | flops 1 | bytes 8 | tf_op jit(solution)/shard_map/pmax | solution.py:96
  96.6 4.6 collective-permute-start.2
  113.9 9.9 fusion.160
  130.4 4.9 collective-permute-start.8
  146.7 10.0 fusion.124
  163.2 5.0 collective-permute-start.14
  180.0 10.0 fusion.93
  196.5 5.1 collective-permute-start.20
  205.7 7.8 collective-permute-start.23
  216.3 10.0 fusion.62
  228.0 658.4 %all-reduce.6.cloned.1.call-done = f32[256,256]{0,1:T(8,128)} async-done(((f32[256,256]{0,1:T(8,128)}), f32[256,256]{0,1:T(8,128)}) %all-reduce.6.cloned.1.call-update) | async-done | bytes 262160 | tf_op jit(solution)/shard_map/psum | solution.py:101
  887.0 45.1 %all-reduce.8.cloned.1.call-done = f32[256,256]{0,1:T(8,128)} async-done(((f32[256,256]{0,1:T(8,128)}), f32[256,256]{0,1:T(8,128)}) %all-reduce.8.cloned.1.call-update) | async-done | bytes 262160 | tf_op jit(solution)/shard_map/psum | solution.py:101
  934.3 11.7 cholesky.130
  946.1 9.8 custom-call.13
  956.3 11.7 cholesky.147
  974.7 19.7 %custom-call.14 = f32[2,128,128]{1,2,0:T(8,128)S(1)} custom-call(f32[2,128,128]{2,1,0:T(8,128)S(1)} %get-tuple-element.19), custom_call_target="InvertDiagBlocksLowerTriangular" | custom-call | tf_op jit(solution)/shard_map/jit(_solve_triangular)/triangular_solve | solution.py:81
  997.7 251.4 %all-reduce.10.cloned.1.call-done = f32[256,256]{0,1:T(8,128)} async-done(((f32[256,256]{0,1:T(8,128)}), f32[256,256]{0,1:T(8,128)}) %all-reduce.10.cloned.1.call-update) | async-done | bytes 262160 | tf_op jit(solution)/shard_map/psum | solution.py:104
  1251.3 11.7 cholesky.164
  1263.1 9.8 custom-call.15
  1273.3 11.7 cholesky.181
  1291.7 19.7 %custom-call.16 = f32[2,128,128]{1,2,0:T(8,128)S(1)} custom-call(f32[2,128,128]{2,1,0:T(8,128)S(1)} %get-tuple-element.20), custom_call_target="InvertDiagBlocksLowerTriangular" | custom-call | tf_op jit(solution)/shard_map/jit(_solve_triangular)/triangular_solve | solution.py:81
  1319.5 4.6 collective-permute-start.26
  1336.3 9.9 fusion.31
  1348.0 260.0 %all-reduce.12.cloned.1.call-done = f32[256,256]{0,1:T(8,128)} async-done(((f32[256,256]{0,1:T(8,128)}), f32[256,256]{0,1:T(8,128)}) %all-reduce.12.cloned.1.call-update) | async-done | bytes 262160 | tf_op jit(solution)/shard_map/psum | solution.py:108
  (155 shorter events, 120.9 us)
Async XLA Ops:
  7.2 879.3 %all-reduce.6.cloned.1.call-start = ((), (), s32[]{:S(2)}) async-start(), calls=%async_computation | async-start | bytes 524288 | tf_op jit(solution)/shard_map/psum | solution.py:101
  8.1 86.0 %collective-permute-start = (f32[1,8,8,256]{3,2,1,0:T(8,128)S(1)}, f32[1,8,8,256]{3,2,1,0:T(8,128)S(1)}, u32[]{:S(2)}, u32[]{:S(2)}) collective-permute-start(f32[1,8,8,256]{3,2,1,0:T(8,128)S(1)} %get-tuple-element.93), channel_id=1, source_target_pairs={{0,64},{64,128},{128,192},{1,65},{65,129},{129,193},{2,66},{66,130... | collective-permute-start | bytes 196616 | tf_op jit(solution)/shard_map/ppermute | solution.py:14
  11.2 84.0 %collective-permute-start.1 = (f32[1,8,8,256]{3,2,1,0:T(8,128)S(1)}, f32[1,8,8,256]{3,2,1,0:T(8,128)S(1)}, u32[]{:S(2)}, u32[]{:S(2)}) collective-permute-start(f32[1,8,8,256]{3,2,1,0:T(8,128)S(1)} %get-tuple-element.92), channel_id=1, source_target_pairs={{64,0},{128,64},{192,128},{65,1},{129,65},{193,129},{66,2},{130,66... | collective-permute-start | bytes 196616 | tf_op jit(solution)/shard_map/ppermute | solution.py:17
  95.3 7.8 collective-permute-start.3
  96.6 6.6 collective-permute-start.2
  103.3 6.6 collective-permute-start.4
  106.9 6.6 collective-permute-start.5
  129.1 7.3 collective-permute-start.9
  130.4 7.2 collective-permute-start.8
  161.9 6.8 collective-permute-start.15
  163.2 7.1 collective-permute-start.14
  170.4 6.8 collective-permute-start.16
  172.3 7.2 collective-permute-start.17
  195.2 6.9 collective-permute-start.21
  196.5 7.2 collective-permute-start.20
  203.8 10.5 collective-permute-start.22
  205.7 10.1 collective-permute-start.23
  228.0 704.2 %all-reduce.8.cloned.1.call-start = ((), (), s32[]{:S(2)}) async-start(), calls=%async_computation.1 | async-start | bytes 524288 | tf_op jit(solution)/shard_map/psum | solution.py:101
  886.5 362.7 %all-reduce.10.cloned.1.call-start = ((), (), s32[]{:S(2)}) async-start(), calls=%async_computation.2 | async-start | bytes 524288 | tf_op jit(solution)/shard_map/psum | solution.py:104
  997.7 610.3 %all-reduce.12.cloned.1.call-start = ((), (), s32[]{:S(2)}) async-start(), calls=%async_computation.3 | async-start | bytes 524288 | tf_op jit(solution)/shard_map/psum | solution.py:108
  1318.2 7.1 collective-permute-start.27
  1319.5 7.2 collective-permute-start.26
  1326.8 6.6 collective-permute-start.28
  1329.1 6.8 collective-permute-start.29
  (14 other events, 181.5 us)
Sparse Core Ops, SparseCore 0:
  228.1 658.3 all-reduce.5
  889.3 42.8 all-reduce.7
  997.8 251.3 all-reduce.9
  1348.1 259.8 all-reduce.11
